TPU v7x, 256 devices: a whole 4x4x8 slice. The times are simulated.
256 devices in a mesh: expert: 16 (over z_hi, x, core), replica: 16 (over z_lo, y).
Axes of the slice: x: 4, y: 4, z: 8 (z_hi: 2, z_lo: 4; z = z_hi * 4 + z_lo), core: 2. Of those that a mesh axis runs over, the one named last changes fastest.
Arguments:
- tokens: bfloat16 [16, 4096, 2048], P('replica', 'expert'), may hold values from -6 to 6
- out_grad: bfloat16 [16, 4096, 2048], P('replica', 'expert'), may hold values from -6 to 6
- routes: int32 [16, 4096, 2], P('replica', 'expert'), may hold values from 0 to 15, all different within a row; in each aligned block of 256 rows (0 to 255, 256 to 511, ..., all dimensions but the last counted through in order) at most 64 rows name the same one
- route_weight: bfloat16 [16, 4096, 2], P('replica', 'expert'), may hold values from 0.19921875 to 1
- gate_up_matrix: bfloat16 [16, 16, 2048, 512], P('replica', 'expert'), may hold values from -6 to 6
- down_matrix: bfloat16 [16, 16, 2048, 256], P('replica', 'expert'), may hold values from -6 to 6
- gate_up_velocity: bfloat16 [16, 16, 2048, 512], P('replica', 'expert'), may hold values from -6 to 6
- down_velocity: bfloat16 [16, 16, 2048, 256], P('replica', 'expert'), may hold values from -6 to 6
- partner: int32 [16], replicated, may hold values from 0 to 15, as said below
Outputs:
- token_grad: bfloat16 [16, 4096, 2048], P('replica', 'expert')
- mixed_gate_up: bfloat16 [16, 16, 2048, 512], P('replica', 'expert')
- mixed_down: bfloat16 [16, 16, 2048, 256], P('replica', 'expert')
Inputs may be any that keep to these rules, and one draw needn't show every extreme that they name: `routes`: the rows of one device route at most 64 pairs to any one expert; no row names an expert twice. partner[r] = r xor s for one power of two s below 16, the same s for all r, so replicas are matched in pairs.
All inputs are finite; a program needn't handle non-finite values.
Results may differ from a plain program's by a relative error of at most 0.0065.
Values may be sent and summed in bfloat16 or wider, within the bound.
A program may use at most 128 MiB of HBM per device.

v0:
```python
import math

import jax
import jax.numpy as jnp
from jax import lax
from jax.sharding import PartitionSpec as P

step_size = 0.2
momentum_decay = 0.9


def shortened(value):

    def short(part):
        return part.astype(jnp.bfloat16) if part.dtype == jnp.float32 else part

    return jax.tree.map(short, value)


def partner_2(block, axis, bit):
    count = lax.axis_size(axis)
    route = []
    for low in range(count):
        high = low | 1 << bit
        if high != low and high < count:
            route += [(low, high), (high, low)]
    return lax.ppermute(block, axis, route)


def in_one_piece(arrays, axis, split_dim, concat_dim, along):
    both = jnp.concatenate(arrays, axis=along)
    out, at, outs = (
        lax.all_to_all(both, axis, split_axis=split_dim, concat_axis=concat_dim, tiled=True),
        0,
        [],
    )
    for a in arrays:
        outs.append(lax.slice_in_dim(out, at, at + a.shape[along], axis=along))
        at += a.shape[along]
    return tuple(outs)


def contract_leading(left, right):
    return lax.dot_general(
        left, right, (((0,), (0,)), ((), ())), preferred_element_type=jnp.float32
    )


def swap_level(value, level):
    return jax.tree.map(
        lambda part, own: part.astype(own.dtype),
        partner_2(shortened(value), "replica", level),
        value,
    )


def per_device(
    tokens,
    out_grad,
    routes,
    route_weight,
    gate_up_matrix,
    down_matrix,
    gate_up_velocity,
    down_velocity,
    partner,
):
    expert_count = lax.axis_size("expert")
    tok_rows = tokens.shape[1]
    top_count = routes.shape[2]
    feature_width = tokens.shape[2]
    hidden_width = down_matrix.shape[3]
    capacity = 2 * tok_rows * top_count // expert_count
    slot_total = expert_count * capacity
    inv_width = 1.0 / math.sqrt(feature_width)
    inverse_hidden = 1.0 / math.sqrt(hidden_width)
    flat_ids = routes[0].reshape(-1)
    onehot = (flat_ids[:, None] == jnp.arange(expert_count, dtype=jnp.int32)[None, :]).astype(
        jnp.int32
    )
    ranks = jnp.sum((jnp.cumsum(onehot, axis=0) - onehot) * onehot, axis=1)
    slot_lookup = flat_ids * capacity + ranks
    chosen = (slot_lookup[None, :] == jnp.arange(slot_total, dtype=jnp.int32)[:, None]).reshape(
        slot_total, tok_rows, top_count
    )
    picker = jnp.any(chosen, axis=2).astype(jnp.bfloat16)
    weighted = jnp.sum(
        jnp.where(chosen, route_weight[0][None, :, :], jnp.zeros((), jnp.bfloat16)), axis=2
    )
    sent_inputs = jnp.dot(picker, tokens[0], preferred_element_type=jnp.float32).astype(
        jnp.bfloat16
    )
    sent_grads = jnp.dot(weighted, out_grad[0], preferred_element_type=jnp.float32).astype(
        jnp.bfloat16
    )
    recv_inputs, received_gradients = in_one_piece(
        (
            sent_inputs.reshape(expert_count, capacity, feature_width),
            sent_grads.reshape(expert_count, capacity, feature_width),
        ),
        "expert",
        0,
        0,
        1,
    )
    input_buffer = recv_inputs.reshape(slot_total, feature_width)
    gradient_buffer = received_gradients.reshape(slot_total, feature_width)
    weight_gu = gate_up_matrix[0, 0]
    down_projection_weight = down_matrix[0, 0]
    pre = jnp.dot(input_buffer, weight_gu, preferred_element_type=jnp.float32) * inv_width
    gate = pre[:, :hidden_width]
    upper = pre[:, hidden_width:]
    active = jax.nn.silu(gate)
    hidden_state = (active * upper).astype(jnp.bfloat16)
    hidden_gradient = (
        jnp.dot(gradient_buffer, down_projection_weight, preferred_element_type=jnp.float32)
        * inverse_hidden
    )
    sigmoid_gate = jax.nn.sigmoid(gate)
    slope = sigmoid_gate * (1.0 + gate * (1.0 - sigmoid_gate))
    pre_grad = jnp.concatenate(
        [hidden_gradient * upper * slope, hidden_gradient * active], axis=1
    ).astype(jnp.bfloat16)
    down_gradient = contract_leading(gradient_buffer, hidden_state) * inverse_hidden
    gate_up_grad = contract_leading(input_buffer, pre_grad) * inv_width
    new_gu = (
        weight_gu.astype(jnp.float32)
        - step_size * (momentum_decay * gate_up_velocity[0, 0].astype(jnp.float32) + gate_up_grad)
    ).astype(jnp.bfloat16)
    next_down_matrix = (
        down_projection_weight.astype(jnp.float32)
        - step_size * (momentum_decay * down_velocity[0, 0].astype(jnp.float32) + down_gradient)
    ).astype(jnp.bfloat16)
    new_gu, next_down_matrix = (new_gu, next_down_matrix)
    replica_count = lax.axis_size("replica")
    bit_total = replica_count.bit_length() - 1
    offset = jnp.bitwise_xor(partner[0], 0)
    level_index = jnp.zeros((), jnp.int32)
    for bit_index in range(bit_total):
        level_index = level_index + bit_index * jnp.bitwise_and(
            jnp.right_shift(offset, bit_index), 1
        )
    joined = jnp.concatenate([new_gu, next_down_matrix], axis=1)
    branches = [functools_partial_level(level) for level in range(bit_total)]
    moved = lax.switch(level_index, branches, joined)
    mixed = (0.5 * (joined.astype(jnp.float32) + moved.astype(jnp.float32))).astype(jnp.bfloat16)
    mixed_gu = mixed[:, : 2 * hidden_width]
    mixed_dn = mixed[:, 2 * hidden_width :]
    paired_gradient = (
        lax.dot_general(
            pre_grad, weight_gu, (((1,), (1,)), ((), ())), preferred_element_type=jnp.float32
        )
        * inv_width
    ).astype(jnp.bfloat16)
    returned = lax.all_to_all(
        paired_gradient.reshape(expert_count, capacity, feature_width),
        "expert",
        split_axis=0,
        concat_axis=0,
        tiled=True,
    )
    combined = contract_leading(picker, returned.reshape(slot_total, feature_width))
    token_grad = combined.astype(jnp.bfloat16)[None]
    return (token_grad, mixed_gu[None, None], mixed_dn[None, None])


def functools_partial_level(level):

    def apply_swap(value):
        return swap_level(value, level)

    return apply_swap


def solution(mesh):
    placed = (
        P("replica", "expert", None),
        P("replica", "expert", None),
        P("replica", "expert", None),
        P("replica", "expert", None),
        P("replica", "expert", None, None),
        P("replica", "expert", None, None),
        P("replica", "expert", None, None),
        P("replica", "expert", None, None),
        P(),
    )
    return jax.shard_map(
        per_device,
        mesh=mesh,
        in_specs=placed,
        out_specs=(
            P("replica", "expert", None),
            P("replica", "expert", None, None),
            P("replica", "expert", None, None),
        ),
        check_vma=False,
    )
```

profile of v0, /device:TPU:1, one launch (start us, length us, event | category | flops | bytes accessed | tf_op | source)
XLA Modules:
  0.0 417.4 jit_solution(4993934556871104649)
XLA Ops:
  5.2 3.2 convolution_convert_fusion.1
  8.3 3.2 convolution_convert_fusion
  11.6 8.4 %pad_maximum_fusion = bf16[16,128,2048]{2,1,0:T(8,128)(2,1)} fusion(bf16[16,64,2048]{2,1,0:T(8,128)(2,1)} %bitcast.78, bf16[16,64,2048]{2,1,0:T(8,128)(2,1)} %bitcast.77), kind=kLoop, calls=%fused_computation | loop fusion | flops 16777216 | bytes 16777216 | tf_op jit(solution)/shard_map/concatenate | solution.py:31
  19.9 200.4 %all_to_all.10 = bf16[16,128,2048]{2,1,0:T(8,128)(2,1)S(1)} all-to-all(bf16[16,128,2048]{2,1,0:T(8,128)(2,1)} %pad_maximum_fusion), channel_id=1, replica_groups=mesh['expert'=16,'replica'=16] {'expert'}, dimensions={0} | all-to-all | bytes 16777216 | tf_op jit(solution)/shard_map/all_to_all | solution.py:33
  221.9 2.4 fusion.13
  224.8 1.7 multiply_convert_fusion.4
  226.5 4.4 %multiply_convert_fusion = bf16[1024,2048]{1,0:T(8,128)(2,1)} fusion(bf16[1,1,2048,512]{3,2,1,0:T(8,128)(2,1)S(1)} %copy-done.6, bf16[1024,256]{0,1:T(8,128)(2,1)S(1)} %get-tuple-element.30, bf16[1024,256]{0,1:T(8,128)(2,1)S(1)} %get-tuple-element.29), kind=kOutput, calls=%fused_computation.1 | convolution fusion | flops 2153775104 | bytes 7340032 | tf_op jit(solution)/shard_map/dot_general | solution.py:150
  230.9 5.5 %all-to-all-start.1 = ((bf16[16,64,2048]{2,1,0:T(8,128)(2,1)}), bf16[16,64,2048]{2,1,0:T(8,128)(2,1)}, u32[]{:S(2)}, u32[]{:S(2)}) async-start(bf16[16,64,2048]{2,1,0:T(8,128)(2,1)} %bitcast.79), calls=%async_computation.1 | async-start | bytes 8388608 | tf_op jit(solution)/shard_map/all_to_all | solution.py:155
  236.4 2.5 copy.47
  238.9 1.4 copy.46
  240.8 2.4 copy.48
  244.1 4.7 %fusion.6 = bf16[2048,256]{0,1:T(8,128)(2,1)S(1)} fusion(bf16[1024,2048]{1,0:T(8,128)(2,1)} %bitcast.83, bf16[1,1,2048,256]{2,3,1,0:T(8,128)(2,1)S(1)} %copy.49, bf16[1,1,2048,256]{2,3,1,0:T(8,128)(2,1)} %copy.46, f32[1024,512]{0,1:T(8,128)} %copy-done.14), kind=kOutput, calls=%fused_computation.15 | convolution fusion | flops 1079508992 | bytes 9437184 | tf_op jit(solution)/shard_map/dot_general | solution.py:44
  249.8 2.8 fusion.2
  252.6 2.1 pad_maximum_fusion.1
  254.7 4.7 %copy.50 = bf16[2048,768]{1,0:T(8,128)(2,1)} copy(bf16[2048,768]{0,1:T(8,128)(2,1)} %pad_maximum_fusion.1) | data formatting | bytes 6291456 | tf_op jit(solution)/shard_map/concatenate | solution.py:143
  259.4 138.3 %conditional.4 = (bf16[2048,768]{1,0:T(8,128)(2,1)}) conditional(s32[]{:T(128)} %bitcast.16, bf16[2048,768]{1,0:T(8,128)(2,1)} %copy.50, bf16[2048,768]{1,0:T(8,128)(2,1)} %copy.50, bf16[2048,768]{1,0:T(8,128)(2,1)} %copy.50, bf16[2048,768]{1,0:T(8,128)(2,1)} %copy.50), branch_computations={%region_5.6_spmd, %region_6.7_spmd, %region_7.8_spmd, %region_8.9_... | conditional | bytes 12582960
  259.7 138.0 %collective-permute-done.2 = bf16[2048,768]{1,0:T(8,128)(2,1)} collective-permute-done((bf16[2048,768]{1,0:T(8,128)(2,1)}, bf16[2048,768]{1,0:T(8,128)(2,1)}, u32[]{:S(2)}, u32[]{:S(2)}) %collective-permute-start.2) | collective-permute-done | bytes 3145760 | tf_op jit(solution)/shard_map/cond/branch_2_fun/ppermute | solution.py:27
  397.7 4.7 %copy.54 = bf16[2048,768]{0,1:T(8,128)(2,1)} copy(bf16[2048,768]{1,0:T(8,128)(2,1)} %get-tuple-element.31) | data formatting | bytes 6291456 | tf_op jit(solution)/shard_map/conditional.1
  402.5 3.4 multiply_convert_fusion.1
  405.9 1.7 copy-done.2
  407.7 2.5 copy.55
  410.2 1.3 slice_bitcast_fusion.1
  411.6 1.3 copy.56
  412.9 4.5 %fusion.7 = bf16[1,256,2048]{2,1,0:T(8,128)(2,1)} fusion(pred[1024,256]{1,0:T(8,128)(4,1)S(1)} %fusion.12, bf16[1024,2048]{1,0:T(8,128)(2,1)} %bitcast.12), kind=kOutput, calls=%fused_computation.16 | convolution fusion | flops 1074266112 | bytes 5505024 | tf_op jit(solution)/shard_map/dot_general | solution.py:44
  (56 shorter events, 9.1 us)
Async XLA Ops:
  0.6 4.5 %copy-start = (bf16[1,256,2048]{2,1,0:T(8,128)(2,1)S(1)}, bf16[1,256,2048]{2,1,0:T(8,128)(2,1)}, u32[]{:S(2)}) copy-start(bf16[1,256,2048]{2,1,0:T(8,128)(2,1)} %param.13) | copy-start | bytes 3145732
  5.1 3.2 copy-start.12
  220.3 1.6 copy-start.6
  221.5 2.8 copy-start.3
  221.5 3.2 copy-start.5
  221.9 2.8 copy-start.10
  224.4 2.1 copy-start.14
  226.5 4.4 %copy-start.15 = (bf16[1024,256]{0,1:T(8,128)(2,1)}, bf16[1024,256]{0,1:T(8,128)(2,1)S(1)}, u32[]{:S(2)}) copy-start(bf16[1024,256]{0,1:T(8,128)(2,1)S(1)} %get-tuple-element.29) | copy-start | bytes 1572868
  226.5 4.4 %copy-start.17 = (bf16[1024,256]{0,1:T(8,128)(2,1)}, bf16[1024,256]{0,1:T(8,128)(2,1)S(1)}, u32[]{:S(2)}) copy-start(bf16[1024,256]{0,1:T(8,128)(2,1)S(1)} %get-tuple-element.30) | copy-start | bytes 1572868
  230.9 182.0 %all-to-all-start.1 = ((bf16[16,64,2048]{2,1,0:T(8,128)(2,1)}), bf16[16,64,2048]{2,1,0:T(8,128)(2,1)}, u32[]{:S(2)}, u32[]{:S(2)}) async-start(bf16[16,64,2048]{2,1,0:T(8,128)(2,1)} %bitcast.79), calls=%async_computation.1 | async-start | bytes 8388608 | tf_op jit(solution)/shard_map/all_to_all | solution.py:155
  238.9 2.0 copy-start.7
  240.8 2.5 copy-start.11
  240.8 3.1 copy-start.13
  244.1 4.8 %copy-start.4 = (bf16[16,64,2048]{2,1,0:T(8,128)(2,1)S(1)}, bf16[16,64,2048]{2,1,0:T(8,128)(2,1)}, u32[]{:S(2)}) copy-start(bf16[16,64,2048]{2,1,0:T(8,128)(2,1)} %copy-done.3) | copy-start | bytes 12582916
  244.1 5.0 %copy-start.8 = (bf16[1,1,2048,512]{2,3,1,0:T(8,128)(2,1)S(1)}, bf16[1,1,2048,512]{2,3,1,0:T(8,128)(2,1)}, u32[]{:S(2)}) copy-start(bf16[1,1,2048,512]{2,3,1,0:T(8,128)(2,1)} %copy.47) | copy-start | bytes 6291460
  244.1 5.6 %copy-start.9 = (bf16[1,1,2048,512]{2,3,1,0:T(8,128)(2,1)S(1)}, bf16[1,1,2048,512]{2,3,1,0:T(8,128)(2,1)}, u32[]{:S(2)}) copy-start(bf16[1,1,2048,512]{2,3,1,0:T(8,128)(2,1)} %copy.48) | copy-start | bytes 6291460
  244.1 5.6 %copy-start.16 = (bf16[1024,256]{0,1:T(8,128)(2,1)S(1)}, bf16[1024,256]{0,1:T(8,128)(2,1)}, u32[]{:S(2)}) copy-start(bf16[1024,256]{0,1:T(8,128)(2,1)} %copy-done.15) | copy-start | bytes 1572868
  244.1 5.8 %copy-start.18 = (bf16[1024,256]{0,1:T(8,128)(2,1)S(1)}, bf16[1024,256]{0,1:T(8,128)(2,1)}, u32[]{:S(2)}) copy-start(bf16[1024,256]{0,1:T(8,128)(2,1)} %copy-done.17) | copy-start | bytes 1572868
  259.4 138.3 %collective-permute-start.2 = (bf16[2048,768]{1,0:T(8,128)(2,1)}, bf16[2048,768]{1,0:T(8,128)(2,1)}, u32[]{:S(2)}, u32[]{:S(2)}) collective-permute-start(bf16[2048,768]{1,0:T(8,128)(2,1)} %param.2), channel_id=1, source_target_pairs={{0,4},{4,0},{1,5},{5,1},{2,6},{6,2},{3,7},{7,3},{8,12},{12,8},{9,1... | collective-permute-start | bytes 9437192 | tf_op jit(solution)/shard_map/cond/branch_2_fun/ppermute | solution.py:27
  405.9 1.7 copy-start.2
  412.9 4.5 %copy-start.1 = (bf16[1,256,2048]{2,1,0:T(8,128)(2,1)S(1)}, bf16[1,256,2048]{2,1,0:T(8,128)(2,1)}, u32[]{:S(2)}) copy-start(bf16[1,256,2048]{2,1,0:T(8,128)(2,1)} %param.13) | copy-start | bytes 3145732
where the time goes:
time: 423 us; the launch traced here: 417 us
  blocking collectives  200 us (47%)
  waiting for transfers between devices  138 us (33%)
  local copies, waits for them, and re-layouts  28.6 us (7%)
  matrix products  27 us (6%)
  other arithmetic  16.6 us (4%)
  starting transfers between devices  5.84 us (1%)
    all_to_all x1, blocking collectives, in_one_piece(): lax.all_to_all(both, axis, split_axis=split_dim, concat_axis=concat_dim,...  200 us
    ppermute x1, waiting for transfers between devices, partner_2(): return lax.ppermute(block, axis, route)  138 us
    unnamed x45, local copies, waits for them, and re-layouts  15.8 us
    dot_general x3, matrix products, contract_leading(): lax.dot_general(left, right, (((0,), (0,)), ((), ())), preferred_element_...  12.1 us
  transfers between devices with their start and end apart: 2, of which 1 were waited for; matrix products, arithmetic and copies ran while one was open for 8% of the time, Pallas kernels for 0%

commit v1 on v0

v1 whole, which is shorter than its diff:
```python
import functools
import math

import jax
import jax.numpy as jnp
from jax import lax
from jax.experimental import pallas as pl
from jax.experimental.pallas import tpu as pltpu
from jax.sharding import PartitionSpec as P

STEP = 0.2
DECAY = 0.9
MESH = pl.DeviceIdType.MESH
CHUNKS = 4
AHEAD = 3
BF16 = jnp.bfloat16
F32 = jnp.float32


def matmul(left, right, left_dim=1, right_dim=0):
    return lax.dot_general(
        left, right, (((left_dim,), (right_dim,)), ((), ())), preferred_element_type=F32
    )


def layer_kernel(
    shift,
    experts,
    info,
    tokens,
    grads,
    gate_up,
    down,
    gate_up_velocity,
    down_velocity,
    token_grad,
    mixed_gate_up,
    mixed_down,
    other_info,
    own_rows,
    other_rows,
    picks,
    packed,
    rows,
    w_gu,
    w_dn,
    v_gu,
    v_dn,
    factors,
    hidden,
    hidden_grad,
    pre_grad,
    new_gu,
    new_dn,
    far_gu,
    far_dn,
    returned,
    across,
    arrived,
    kept,
    load_sem,
    store_sem,
    z_send,
    z_recv,
    x_send,
    x_recv,
    ret_send,
    ret_recv,
    back_send,
    back_recv,
    mix_send,
    mix_recv,
):
    tok_rows, width = tokens.shape
    half_width = down.shape[1]
    group = experts // 2
    total = rows.shape[1]
    part_rows = total // 2
    capacity = part_rows // group
    columns = width // CHUNKS
    inv_width = 1.0 / math.sqrt(width)
    inv_hidden = 1.0 / math.sqrt(half_width)

    me = lax.axis_index("expert")
    replica = lax.axis_index("replica")
    side = me // group
    mine = me % group
    opposite = (me + group) % experts
    mate = replica + shift - 2 * shift * ((replica // shift) % 2)

    def member(at):
        return {"expert": side * group + at}

    def span(chunk):
        return pl.ds(chunk * columns, columns)

    def block(part, at):
        return pl.ds(pl.multiple_of(part * part_rows + at * capacity, capacity), capacity)

    barrier = pltpu.get_barrier_semaphore()
    for step in range(1, group):
        pl.semaphore_signal(
            barrier, inc=1, device_id=member((mine + step) % group), device_id_type=MESH
        )
    pl.semaphore_signal(barrier, inc=1, device_id={"expert": opposite}, device_id_type=MESH)
    pl.semaphore_signal(barrier, inc=1, device_id={"replica": mate}, device_id_type=MESH)

    sources = (tokens, grads)
    loads = [
        pltpu.make_async_copy(tokens, own_rows.at[0], load_sem.at[0]),
        pltpu.make_async_copy(grads, own_rows.at[1], load_sem.at[1]),
        pltpu.make_async_copy(gate_up, w_gu, load_sem.at[2]),
        pltpu.make_async_copy(down, w_dn, load_sem.at[3]),
        pltpu.make_async_copy(down_velocity, v_dn, load_sem.at[4]),
        pltpu.make_async_copy(gate_up_velocity, v_gu, load_sem.at[5]),
    ]
    for load in loads:
        load.start()
    pl.semaphore_wait(barrier, group + 1)

    def z_copy(index):
        array, chunk = divmod(index, CHUNKS)
        return pltpu.make_async_remote_copy(
            src_ref=sources[array].at[:, span(chunk)],
            dst_ref=other_rows.at[array, :, span(chunk)],
            send_sem=z_send.at[index],
            recv_sem=z_recv.at[index],
            device_id={"expert": opposite},
            device_id_type=MESH,
        )

    info_copy = pltpu.make_async_remote_copy(
        src_ref=info,
        dst_ref=other_info,
        send_sem=z_send.at[2 * CHUNKS],
        recv_sem=z_recv.at[2 * CHUNKS],
        device_id={"expert": opposite},
        device_id_type=MESH,
    )
    info_copy.start()
    for index in range(AHEAD):
        z_copy(index).start()

    def choose(part, table):
        names = [table[k : k + 1, :] for k in range(2)]
        weights = [table[2 + k : 3 + k, :] for k in range(2)]
        listed = lax.broadcasted_iota(jnp.int32, (experts, tok_rows), 0).astype(F32)
        member_of = jnp.where((names[0] == listed) | (names[1] == listed), 1.0, 0.0)
        earlier = jnp.where(
            lax.broadcasted_iota(jnp.int32, (tok_rows, tok_rows), 0)
            < lax.broadcasted_iota(jnp.int32, (tok_rows, tok_rows), 1),
            1.0,
            0.0,
        )
        before = matmul(member_of.astype(BF16), earlier.astype(BF16))
        first = (side * part_rows).astype(F32)
        slots = [
            name * float(capacity)
            + jnp.sum(jnp.where(name == listed, before, 0.0), axis=0, keepdims=True)
            - first
            for name in names
        ]
        place = lax.broadcasted_iota(jnp.int32, (part_rows, tok_rows), 0).astype(F32)
        hits = [slot == place for slot in slots]
        picks[0, part] = jnp.where(hits[0] | hits[1], 1.0, 0.0).astype(BF16)
        picks[1, part] = (
            jnp.where(hits[0], weights[0], 0.0) + jnp.where(hits[1], weights[1], 0.0)
        ).astype(BF16)

    def pass_on(source, target, part, chunk, send, recv):
        target[block(part, mine), span(chunk)] = source[block(part, mine), span(chunk)]
        for step in range(1, group):
            at = (mine + step) % group
            pltpu.make_async_remote_copy(
                src_ref=source.at[block(part, at), span(chunk)],
                dst_ref=target.at[block(part, mine), span(chunk)],
                send_sem=send,
                recv_sem=recv,
                device_id=member(at),
                device_id_type=MESH,
            ).start()

    def all_sent_or_here(source, target, cut, send, recv):
        some = pl.ds(0, part_rows - capacity)
        return pltpu.make_async_remote_copy(
            src_ref=source.at[some, cut],
            dst_ref=target.at[some, cut],
            send_sem=send,
            recv_sem=recv,
            device_id={"expert": opposite},
            device_id_type=MESH,
        )

    def dispatch(array, part, chunk):
        held = own_rows if part == 0 else other_rows
        picked = matmul(picks[array, part], held[array, :, span(chunk)])
        packed[array, part * part_rows : (part + 1) * part_rows, span(chunk)] = picked.astype(BF16)
        pass_on(
            packed.at[array],
            rows.at[array],
            part,
            chunk,
            x_send.at[2 * array + part],
            x_recv.at[(2 * array + part) * CHUNKS + chunk],
        )

    def wait_rows(array, part, chunk):
        all_sent_or_here(
            packed.at[array],
            rows.at[array],
            span(chunk),
            x_send.at[2 * array + part],
            x_recv.at[(2 * array + part) * CHUNKS + chunk],
        ).wait_recv()

    def forward(part):
        def one(at, carry):
            here = pl.ds(pl.multiple_of(part * part_rows + at * 128, 128), 128)
            pre = matmul(rows[0, here, :], w_gu[...]) * inv_width
            gate = pre[:, :half_width]
            upper = pre[:, half_width:]
            sigmoid = jax.nn.sigmoid(gate)
            active = gate * sigmoid
            hidden[here, :] = (active * upper).astype(BF16)
            factors[here, :half_width] = upper * (sigmoid * (1.0 + gate * (1.0 - sigmoid)))
            factors[here, half_width:] = active
            return carry

        lax.fori_loop(0, part_rows // 128, one, 0)

    choose(0, info)
    loads[0].wait()
    for chunk in range(CHUNKS):
        dispatch(0, 0, chunk)
    loads[1].wait()
    for chunk in range(CHUNKS):
        dispatch(1, 0, chunk)
    info_copy.wait()
    choose(1, other_info)

    def take(index):
        copy = z_copy(index)
        copy.wait_recv()
        copy.wait_send()
        if index + AHEAD < 2 * CHUNKS:
            z_copy(index + AHEAD).start()
        dispatch(index // CHUNKS, 1, index % CHUNKS)

    for index in range(CHUNKS):
        take(index)
        if index == CHUNKS - 2:
            loads[2].wait()
            for chunk in range(CHUNKS):
                wait_rows(0, 0, chunk)
            forward(0)
    loads[3].wait()
    loads[4].wait()
    loads[5].wait()

    def swap_copy(source, target, at, count, index):
        part = pl.ds(at * count, count)
        return pltpu.make_async_remote_copy(
            src_ref=source.at[part],
            dst_ref=target.at[part],
            send_sem=mix_send.at[index],
            recv_sem=mix_recv.at[index],
            device_id={"replica": mate},
            device_id_type=MESH,
        )

    def stepped(weight, velocity, gradient):
        return (
            weight.astype(F32) - STEP * (DECAY * velocity.astype(F32) + gradient)
        ).astype(BF16)

    def down_chunk(chunk):
        wait_rows(1, 0, chunk)
        wait_rows(1, 1, chunk)
        here = pl.ds(chunk * columns, columns)

        def one(at, carry):
            those = pl.ds(pl.multiple_of(at * 256, 256), 256)
            term = matmul(rows[1, those, span(chunk)], w_dn[here, :])
            if chunk == 0:
                hidden_grad[those, :] = term
            else:
                hidden_grad[those, :] += term
            return carry

        lax.fori_loop(0, total // 256, one, 0)
        gradient = matmul(rows[1, :, span(chunk)], hidden[...], 0, 0) * inv_hidden
        new_dn[here, :] = stepped(w_dn[here, :], v_dn[here, :], gradient)
        swap_copy(new_dn, far_dn, chunk, columns, CHUNKS + chunk).start()

    for index in range(CHUNKS):
        take(CHUNKS + index)
        if index == 1:
            for chunk in range(CHUNKS):
                wait_rows(0, 1, chunk)
            forward(1)
        if index >= 2:
            down_chunk(index - 2)
    for chunk in range(CHUNKS - 2, CHUNKS):
        down_chunk(chunk)

    def finish(at, carry):
        here = pl.ds(pl.multiple_of(at * 128, 128), 128)
        scaled = hidden_grad[here, :] * inv_hidden
        pre_grad[here, :half_width] = (scaled * factors[here, :half_width]).astype(BF16)
        pre_grad[here, half_width:] = (scaled * factors[here, half_width:]).astype(BF16)
        return carry

    lax.fori_loop(0, total // 128, finish, 0)

    for part in range(2):
        all_sent_or_here(
            packed.at[0], rows.at[0], slice(None), x_send.at[part], x_recv.at[0]
        ).wait_send()

    def give_back(part, chunk):
        here = pl.ds(chunk * columns, columns)
        base = part * part_rows

        def one(at, carry):
            those = pl.ds(pl.multiple_of(base + at * 256, 256), 256)
            pair = matmul(pre_grad[those, :], w_gu[here, :], 1, 1) * inv_width
            packed[0, those, span(chunk)] = pair.astype(BF16)
            return carry

        lax.fori_loop(0, part_rows // 256, one, 0)
        pass_on(
            packed.at[0],
            returned,
            part,
            chunk,
            ret_send.at[part],
            ret_recv.at[part * CHUNKS + chunk],
        )

    def gate_up_chunk(chunk):
        here = pl.ds(chunk * columns, columns)
        gradient = matmul(rows[0, :, span(chunk)], pre_grad[...], 0, 0) * inv_width
        new_gu[here, :] = stepped(w_gu[here, :], v_gu[here, :], gradient)
        swap_copy(new_gu, far_gu, chunk, columns, chunk).start()

    for chunk in range(CHUNKS):
        give_back(1, chunk)
        gate_up_chunk(chunk)

    def wait_back(part, chunk):
        all_sent_or_here(
            packed.at[0],
            returned,
            span(chunk),
            ret_send.at[part],
            ret_recv.at[part * CHUNKS + chunk],
        ).wait_recv()

    def combine(part, chunk):
        wait_back(part, chunk)
        there = returned[part * part_rows : (part + 1) * part_rows, span(chunk)]
        return matmul(picks[0, part], there, 0, 0).astype(BF16)

    def back_copy(chunk):
        return pltpu.make_async_remote_copy(
            src_ref=across.at[:, span(chunk)],
            dst_ref=arrived.at[:, span(chunk)],
            send_sem=back_send.at[chunk],
            recv_sem=back_recv.at[chunk],
            device_id={"expert": opposite},
            device_id_type=MESH,
        )

    for chunk in range(CHUNKS):
        across[:, span(chunk)] = combine(1, chunk)
        back_copy(chunk).start()
        give_back(0, chunk)
    for chunk in range(CHUNKS):
        kept[:, span(chunk)] = combine(0, chunk)

    stores = []

    def mix(own, far, result, chunk, index):
        copy = swap_copy(own, far, chunk, columns, index)
        copy.wait_recv()
        here = pl.ds(chunk * columns, columns)
        far[here, :] = (0.5 * (own[here, :].astype(F32) + far[here, :].astype(F32))).astype(BF16)
        store = pltpu.make_async_copy(far.at[here], result.at[here], store_sem.at[index])
        store.start()
        stores.append(store)
        copy.wait_send()

    for chunk in range(CHUNKS):
        mix(new_dn, far_dn, mixed_down, chunk, CHUNKS + chunk)
    for chunk in range(CHUNKS):
        mix(new_gu, far_gu, mixed_gate_up, chunk, chunk)
    for chunk in range(CHUNKS):
        copy = back_copy(chunk)
        copy.wait_recv()
        both = kept[:, span(chunk)].astype(F32) + arrived[:, span(chunk)].astype(F32)
        kept[:, span(chunk)] = both.astype(BF16)
        store = pltpu.make_async_copy(
            kept.at[:, span(chunk)], token_grad.at[:, span(chunk)], store_sem.at[2 * CHUNKS + chunk]
        )
        store.start()
        stores.append(store)
        copy.wait_send()
    for part in range(2):
        all_sent_or_here(
            packed.at[1], rows.at[1], slice(None), x_send.at[2 + part], x_recv.at[0]
        ).wait_send()
        all_sent_or_here(
            packed.at[0], returned, slice(None), ret_send.at[part], ret_recv.at[0]
        ).wait_send()
    for store in stores:
        store.wait()


def layer(level, experts, info, *arrays):
    tokens, _, gate_up, down = arrays[:4]
    tok_rows, width = tokens.shape
    twice = gate_up.shape[1]
    single = down.shape[1]
    total = 2 * tok_rows * 2
    part_rows = total // 2
    vmem = pltpu.VMEM
    sems = pltpu.SemaphoreType.DMA
    anywhere = pl.BlockSpec(memory_space=pl.ANY)
    return pl.pallas_call(
        functools.partial(layer_kernel, 1 << level, experts),
        out_shape=(
            jax.ShapeDtypeStruct((tok_rows, width), BF16),
            jax.ShapeDtypeStruct((width, twice), BF16),
            jax.ShapeDtypeStruct((width, single), BF16),
        ),
        in_specs=[pl.BlockSpec(memory_space=pltpu.VMEM)] + [anywhere] * 6,
        out_specs=(anywhere,) * 3,
        scratch_shapes=[
            vmem(info.shape, F32),
            vmem((2, tok_rows, width), BF16),
            vmem((2, tok_rows, width), BF16),
            vmem((2, 2, part_rows, tok_rows), BF16),
            vmem((2, total, width), BF16),
            vmem((2, total, width), BF16),
            vmem((width, twice), BF16),
            vmem((width, single), BF16),
            vmem((width, twice), BF16),
            vmem((width, single), BF16),
            vmem((total, twice), F32),
            vmem((total, single), BF16),
            vmem((total, single), F32),
            vmem((total, twice), BF16),
            vmem((width, twice), BF16),
            vmem((width, single), BF16),
            vmem((width, twice), BF16),
            vmem((width, single), BF16),
            vmem((total, width), BF16),
            vmem((tok_rows, width), BF16),
            vmem((tok_rows, width), BF16),
            vmem((tok_rows, width), BF16),
            sems((6,)),
            sems((3 * CHUNKS,)),
            sems((2 * CHUNKS + 1,)),
            sems((2 * CHUNKS + 1,)),
            sems((4,)),
            sems((4 * CHUNKS,)),
            sems((2,)),
            sems((2 * CHUNKS,)),
            sems((CHUNKS,)),
            sems((CHUNKS,)),
            sems((2 * CHUNKS,)),
            sems((2 * CHUNKS,)),
        ],
        name=f"layer_shift_{1 << level}",
        compiler_params=pltpu.CompilerParams(
            collective_id=level, has_side_effects=True, vmem_limit_bytes=60 << 20
        ),
    )(info, *arrays)


def per_device(
    tokens,
    out_grad,
    routes,
    route_weight,
    gate_up_matrix,
    down_matrix,
    gate_up_velocity,
    down_velocity,
    partner,
):
    experts = lax.axis_size("expert")
    levels = lax.axis_size("replica").bit_length() - 1
    info = jnp.concatenate(
        [
            routes[0].T.astype(F32),
            route_weight[0].T.astype(F32),
            jnp.zeros((4, tokens.shape[1]), F32),
        ],
        axis=0,
    )
    shift = partner[0]
    level = jnp.zeros((), jnp.int32)
    for bit in range(levels):
        level = level + bit * jnp.bitwise_and(jnp.right_shift(shift, bit), 1)
    token_grad, mixed_gate_up, mixed_down = lax.switch(
        level,
        [functools.partial(layer, at, experts) for at in range(levels)],
        info,
        tokens[0],
        out_grad[0],
        gate_up_matrix[0, 0],
        down_matrix[0, 0],
        gate_up_velocity[0, 0],
        down_velocity[0, 0],
    )
    return token_grad[None], mixed_gate_up[None, None], mixed_down[None, None]


def solution(mesh):
    row = P("replica", "expert", None)
    weight = P("replica", "expert", None, None)
    return jax.shard_map(
        per_device,
        mesh=mesh,
        in_specs=(row,) * 4 + (weight,) * 4 + (P(),),
        out_specs=(row, weight, weight),
        check_vma=False,
    )
```

time: 423 us -> 302 us (0.71)
  Pallas kernels: 0 us -> 284 us
  blocking collectives: 200 us -> 0 us
  waiting for transfers between devices: 138 us -> 0 us
  matrix products: 27 us -> 0 us
  local copies, waits for them, and re-layouts: 28.6 us -> 3.98 us
  other arithmetic: 16.6 us -> 1.44 us
  loops' own time: 0.01 us -> 6.73 us
  starting transfers between devices: 5.84 us -> 0 us
    pallas_call x0 -> x1, Pallas kernels: none -> 284 us  [layer(): pl.pallas_call(functools.partial(layer_kernel, 1 << level, experts), out_...]
    all_to_all x1 -> x0, blocking collectives: 200 us -> none  [in_one_piece(): lax.all_to_all(both, axis, split_axis=split_dim, concat_axis=concat_dim,...]
    ppermute x1 -> x0, waiting for transfers between devices: 138 us -> none  [partner_2(): return lax.ppermute(block, axis, route)]
    dot_general x8 -> x0, matrix products: 27 us -> none  [the longest x3 12.1 us: contract_leading(): lax.dot_general(left, right, (((0,), (0,)), ((), ())), preferred_element_...]
    unnamed x45 -> x5, local copies, waits for them, and re-layouts: 15.8 us -> 3.9 us
    concatenate x2 -> x1, other arithmetic: 10.4 us -> 0.07 us  [per_device(): jnp.concatenate([routes[0].T.astype(F32), route_weight[0].T.astype(F32),...]
    another operation x0 -> x1, loops' own time: none -> 6.73 us  [per_device(): lax.switch(level, [functools.partial(layer, at, experts) for at in range(...]
    all_to_all x1 -> x0, starting transfers between devices: 5.53 us -> none  [per_device(): lax.all_to_all(paired_gradient.reshape(expert_count, capacity, feature_wi...]
  transfers between devices with their start and end apart: 2 -> 0, of which waited for: 1 -> 0; matrix products, arithmetic and copies ran while one was open for 8% -> 0% of each run, Pallas kernels for 0% -> 0%
where the time goes in v1:
time: 302 us; the launch traced here: 299 us
  Pallas kernels  284 us (94%)
  loops' own time  6.73 us (2%)
  local copies, waits for them, and re-layouts  3.98 us (1%)
    pallas_call x1, Pallas kernels, layer(): pl.pallas_call(functools.partial(layer_kernel, 1 << level, experts), out_...  284 us
    another operation x1, loops' own time, per_device(): lax.switch(level, [functools.partial(layer, at, experts) for at in range(...  6.73 us

profile of v1, /device:TPU:1, one launch (start us, length us, event | category | flops | bytes accessed | tf_op | source)
XLA Modules:
  0.0 299.4 jit_solution(12631333614896132664)
XLA Ops:
  2.6 0.1 pad.2.clone
  2.7 0.7 convert_bitcast_fusion.1
  3.3 0.7 convert_bitcast_fusion
  4.0 0.1 maximum_maximum_fusion
  4.1 291.1 %conditional.1 = ((bf16[256,2048]{1,0:T(8,128)(2,1)S(1)}, bf16[2048,512]{1,0:T(8,128)(2,1)S(1)}, bf16[2048,256]{1,0:T(8,128)(2,1)})) conditional(s32[]{:T(128)} %bitcast.24, (bf16[1,256,2048]{2,1,0:T(8,128)(2,1)}, bf16[1,256,2048]{2,1,0:T(8,128)(2,1)}, bf16[1,1,2048,512]{3,2,1,0:T(8,128)(2,1)}, ...), branch_computations={%region_0.0_spmd, %region_1.0_spmd, %region_2.0_spmd, %region_3.0_... | conditional | bytes 8 | solution.py:506
  10.6 284.4 %layer_shift_8.1 = (bf16[256,2048]{1,0:T(8,128)(2,1)S(1)}, bf16[2048,512]{1,0:T(8,128)(2,1)S(1)}, bf16[2048,256]{1,0:T(8,128)(2,1)}) custom-call(f32[8,256]{1,0:T(8,128)S(1)} %get-tuple-element.125.info, bf16[256,2048]{1,0:T(8,128)(2,1)} %bitcast.49, bf16[256,2048]{1,0:T(8,128)(2,1)} %bitcast.53, bf16[2048,512]{1,0:T(8,128)(2,1)} %bitcast.41, ...), custom_call_target="tpu_custom_call" | custom-call | tf_op jit(solution)/shard_map/cond/branch_3_fun/layer_shift_8/pallas_call | solution.py:429
  295.2 1.0 copy.27
  296.2 0.0 copy-start
  296.2 1.3 copy.28
  297.5 0.6 copy-done
  298.2 1.0 copy.29
  (1 shorter events, 0.0 us)
Async XLA Ops:
  296.2 2.0 copy-start

commit v2 on v1

--- a/solution.py
+++ b/solution.py
@@ -13,6 +13,9 @@
 MESH = pl.DeviceIdType.MESH
 CHUNKS = 4
 AHEAD = 3
+FIRST = 2
+FORWARD_GAP = 3
+LATE = 6
 BF16 = jnp.bfloat16
 F32 = jnp.float32
 
@@ -37,8 +40,7 @@
     mixed_gate_up,
     mixed_down,
     other_info,
-    own_rows,
-    other_rows,
+    held,
     picks,
     packed,
     rows,
@@ -57,7 +59,6 @@
     returned,
     across,
     arrived,
-    kept,
     load_sem,
     store_sem,
     z_send,
@@ -92,7 +93,7 @@
         return {"expert": side * group + at}
 
     def span(chunk):
-        return pl.ds(chunk * columns, columns)
+        return pl.ds(pl.multiple_of(chunk * columns, columns), columns)
 
     def block(part, at):
         return pl.ds(pl.multiple_of(part * part_rows + at * capacity, capacity), capacity)
@@ -105,10 +106,9 @@
     pl.semaphore_signal(barrier, inc=1, device_id={"expert": opposite}, device_id_type=MESH)
     pl.semaphore_signal(barrier, inc=1, device_id={"replica": mate}, device_id_type=MESH)
 
-    sources = (tokens, grads)
     loads = [
-        pltpu.make_async_copy(tokens, own_rows.at[0], load_sem.at[0]),
-        pltpu.make_async_copy(grads, own_rows.at[1], load_sem.at[1]),
+        pltpu.make_async_copy(tokens, held.at[0, 0], load_sem.at[0]),
+        pltpu.make_async_copy(grads, held.at[0, 1], load_sem.at[1]),
         pltpu.make_async_copy(gate_up, w_gu, load_sem.at[2]),
         pltpu.make_async_copy(down, w_dn, load_sem.at[3]),
         pltpu.make_async_copy(down_velocity, v_dn, load_sem.at[4]),
@@ -118,11 +118,12 @@
         load.start()
     pl.semaphore_wait(barrier, group + 1)
 
-    def z_copy(index):
-        array, chunk = divmod(index, CHUNKS)
+    def z_copy(index, source=None):
+        array, chunk = index // CHUNKS, index % CHUNKS
+        source = held.at[0, array] if source is None else source
         return pltpu.make_async_remote_copy(
-            src_ref=sources[array].at[:, span(chunk)],
-            dst_ref=other_rows.at[array, :, span(chunk)],
+            src_ref=source.at[:, span(chunk)],
+            dst_ref=held.at[1, array, :, span(chunk)],
             send_sem=z_send.at[index],
             recv_sem=z_recv.at[index],
             device_id={"expert": opposite},
@@ -139,7 +140,7 @@
     )
     info_copy.start()
     for index in range(AHEAD):
-        z_copy(index).start()
+        z_copy(index, tokens).start()
 
     def choose(part, table):
         names = [table[k : k + 1, :] for k in range(2)]
@@ -169,7 +170,8 @@
 
     def pass_on(source, target, part, chunk, send, recv):
         target[block(part, mine), span(chunk)] = source[block(part, mine), span(chunk)]
-        for step in range(1, group):
+
+        def one(step, carry):
             at = (mine + step) % group
             pltpu.make_async_remote_copy(
                 src_ref=source.at[block(part, at), span(chunk)],
@@ -179,6 +181,9 @@
                 device_id=member(at),
                 device_id_type=MESH,
             ).start()
+            return carry
+
+        lax.fori_loop(1, group, one, 0)
 
     def all_sent_or_here(source, target, cut, send, recv):
         some = pl.ds(0, part_rows - capacity)
@@ -191,10 +196,17 @@
             device_id_type=MESH,
         )
 
+    def half_rows(part, at, count):
+        return pl.ds(pl.multiple_of(part * part_rows + at * count, count), count)
+
     def dispatch(array, part, chunk):
-        held = own_rows if part == 0 else other_rows
-        picked = matmul(picks[array, part], held[array, :, span(chunk)])
-        packed[array, part * part_rows : (part + 1) * part_rows, span(chunk)] = picked.astype(BF16)
+        def one(at, carry):
+            slots = pl.ds(pl.multiple_of(at * 128, 128), 128)
+            picked = matmul(picks[array, part, slots, :], held[part, array, :, span(chunk)])
+            packed[array, half_rows(part, at, 128), span(chunk)] = picked.astype(BF16)
+            return carry
+
+        lax.fori_loop(0, part_rows // 128, one, 0)
         pass_on(
             packed.at[array],
             rows.at[array],
@@ -213,9 +225,18 @@
             x_recv.at[(2 * array + part) * CHUNKS + chunk],
         ).wait_recv()
 
+    def each(count, step):
+        def one(at, carry):
+            step(at)
+            return carry
+
+        lax.fori_loop(0, count, one, 0)
+
     def forward(part):
-        def one(at, carry):
-            here = pl.ds(pl.multiple_of(part * part_rows + at * 128, 128), 128)
+        each(CHUNKS, lambda chunk: wait_rows(0, part, chunk))
+
+        def one(at):
+            here = half_rows(part, at, 128)
             pre = matmul(rows[0, here, :], w_gu[...]) * inv_width
             gate = pre[:, :half_width]
             upper = pre[:, half_width:]
@@ -224,41 +245,32 @@
             hidden[here, :] = (active * upper).astype(BF16)
             factors[here, :half_width] = upper * (sigmoid * (1.0 + gate * (1.0 - sigmoid)))
             factors[here, half_width:] = active
-            return carry
-
-        lax.fori_loop(0, part_rows // 128, one, 0)
+            hidden_grad[here, :] = jnp.zeros((128, half_width), F32)
+
+        each(part_rows // 128, one)
 
     choose(0, info)
     loads[0].wait()
-    for chunk in range(CHUNKS):
-        dispatch(0, 0, chunk)
     loads[1].wait()
-    for chunk in range(CHUNKS):
-        dispatch(1, 0, chunk)
+    each(2 * CHUNKS, lambda index: dispatch(index // CHUNKS, 0, index % CHUNKS))
     info_copy.wait()
     choose(1, other_info)
+    for load in loads[2:]:
+        load.wait()
 
     def take(index):
         copy = z_copy(index)
         copy.wait_recv()
         copy.wait_send()
-        if index + AHEAD < 2 * CHUNKS:
+
+        @pl.when(index + AHEAD < 2 * CHUNKS)
+        def _():
             z_copy(index + AHEAD).start()
+
         dispatch(index // CHUNKS, 1, index % CHUNKS)
 
-    for index in range(CHUNKS):
-        take(index)
-        if index == CHUNKS - 2:
-            loads[2].wait()
-            for chunk in range(CHUNKS):
-                wait_rows(0, 0, chunk)
-            forward(0)
-    loads[3].wait()
-    loads[4].wait()
-    loads[5].wait()
-
     def swap_copy(source, target, at, count, index):
-        part = pl.ds(at * count, count)
+        part = pl.ds(pl.multiple_of(at * count, count), count)
         return pltpu.make_async_remote_copy(
             src_ref=source.at[part],
             dst_ref=target.at[part],
@@ -276,41 +288,43 @@
     def down_chunk(chunk):
         wait_rows(1, 0, chunk)
         wait_rows(1, 1, chunk)
-        here = pl.ds(chunk * columns, columns)
-
-        def one(at, carry):
+
+        def term(at):
             those = pl.ds(pl.multiple_of(at * 256, 256), 256)
-            term = matmul(rows[1, those, span(chunk)], w_dn[here, :])
-            if chunk == 0:
-                hidden_grad[those, :] = term
-            else:
-                hidden_grad[those, :] += term
-            return carry
-
-        lax.fori_loop(0, total // 256, one, 0)
-        gradient = matmul(rows[1, :, span(chunk)], hidden[...], 0, 0) * inv_hidden
-        new_dn[here, :] = stepped(w_dn[here, :], v_dn[here, :], gradient)
+            hidden_grad[those, :] += matmul(rows[1, those, span(chunk)], w_dn[span(chunk), :])
+
+        each(total // 256, term)
+
+        def update(at):
+            here = pl.ds(pl.multiple_of(chunk * columns + at * 256, 256), 256)
+            gradient = matmul(rows[1, :, here], hidden[...], 0, 0) * inv_hidden
+            new_dn[here, :] = stepped(w_dn[here, :], v_dn[here, :], gradient)
+
+        each(columns // 256, update)
         swap_copy(new_dn, far_dn, chunk, columns, CHUNKS + chunk).start()
 
-    for index in range(CHUNKS):
-        take(CHUNKS + index)
-        if index == 1:
-            for chunk in range(CHUNKS):
-                wait_rows(0, 1, chunk)
-            forward(1)
-        if index >= 2:
-            down_chunk(index - 2)
-    for chunk in range(CHUNKS - 2, CHUNKS):
-        down_chunk(chunk)
-
-    def finish(at, carry):
+    def dispatch_step(index):
+        @pl.when(index < 2 * CHUNKS)
+        def _():
+            take(index)
+
+        @pl.when((index == FIRST) | (index == FIRST + FORWARD_GAP))
+        def _():
+            forward((index - FIRST) // FORWARD_GAP)
+
+        @pl.when(index >= LATE)
+        def _():
+            down_chunk(index - LATE)
+
+    each(LATE + CHUNKS, dispatch_step)
+
+    def finish(at):
         here = pl.ds(pl.multiple_of(at * 128, 128), 128)
         scaled = hidden_grad[here, :] * inv_hidden
         pre_grad[here, :half_width] = (scaled * factors[here, :half_width]).astype(BF16)
         pre_grad[here, half_width:] = (scaled * factors[here, half_width:]).astype(BF16)
-        return carry
-
-    lax.fori_loop(0, total // 128, finish, 0)
+
+    each(total // 128, finish)
 
     for part in range(2):
         all_sent_or_here(
@@ -318,16 +332,12 @@
         ).wait_send()
 
     def give_back(part, chunk):
-        here = pl.ds(chunk * columns, columns)
-        base = part * part_rows
-
-        def one(at, carry):
-            those = pl.ds(pl.multiple_of(base + at * 256, 256), 256)
-            pair = matmul(pre_grad[those, :], w_gu[here, :], 1, 1) * inv_width
+        def one(at):
+            those = half_rows(part, at, 256)
+            pair = matmul(pre_grad[those, :], w_gu[span(chunk), :], 1, 1) * inv_width
             packed[0, those, span(chunk)] = pair.astype(BF16)
-            return carry
-
-        lax.fori_loop(0, part_rows // 256, one, 0)
+
+        each(part_rows // 256, one)
         pass_on(
             packed.at[0],
             returned,
@@ -338,14 +348,13 @@
         )
 
     def gate_up_chunk(chunk):
-        here = pl.ds(chunk * columns, columns)
-        gradient = matmul(rows[0, :, span(chunk)], pre_grad[...], 0, 0) * inv_width
-        new_gu[here, :] = stepped(w_gu[here, :], v_gu[here, :], gradient)
+        def update(at):
+            here = pl.ds(pl.multiple_of(chunk * columns + at * 256, 256), 256)
+            gradient = matmul(rows[0, :, here], pre_grad[...], 0, 0) * inv_width
+            new_gu[here, :] = stepped(w_gu[here, :], v_gu[here, :], gradient)
+
+        each(columns // 256, update)
         swap_copy(new_gu, far_gu, chunk, columns, chunk).start()
-
-    for chunk in range(CHUNKS):
-        give_back(1, chunk)
-        gate_up_chunk(chunk)
 
     def wait_back(part, chunk):
         all_sent_or_here(
@@ -358,12 +367,12 @@
 
     def combine(part, chunk):
         wait_back(part, chunk)
-        there = returned[part * part_rows : (part + 1) * part_rows, span(chunk)]
-        return matmul(picks[0, part], there, 0, 0).astype(BF16)
+        there = returned[half_rows(part, 0, part_rows), span(chunk)]
+        across[part, :, span(chunk)] = matmul(picks[0, part], there, 0, 0).astype(BF16)
 
     def back_copy(chunk):
         return pltpu.make_async_remote_copy(
-            src_ref=across.at[:, span(chunk)],
+            src_ref=across.at[1, :, span(chunk)],
             dst_ref=arrived.at[:, span(chunk)],
             send_sem=back_send.at[chunk],
             recv_sem=back_recv.at[chunk],
@@ -371,40 +380,48 @@
             device_id_type=MESH,
         )
 
-    for chunk in range(CHUNKS):
-        across[:, span(chunk)] = combine(1, chunk)
-        back_copy(chunk).start()
-        give_back(0, chunk)
-    for chunk in range(CHUNKS):
-        kept[:, span(chunk)] = combine(0, chunk)
-
-    stores = []
+    def return_step(index):
+        @pl.when(index < 2 * CHUNKS)
+        def _():
+            give_back(1 - index // CHUNKS, index % CHUNKS)
+
+        @pl.when(index < CHUNKS)
+        def _():
+            gate_up_chunk(index)
+
+        @pl.when(index >= CHUNKS)
+        def _():
+            combine(2 - index // CHUNKS, index % CHUNKS)
+
+        @pl.when((index >= CHUNKS) & (index < 2 * CHUNKS))
+        def _():
+            back_copy(index % CHUNKS).start()
+
+    each(3 * CHUNKS, return_step)
 
     def mix(own, far, result, chunk, index):
         copy = swap_copy(own, far, chunk, columns, index)
         copy.wait_recv()
-        here = pl.ds(chunk * columns, columns)
+        here = span(chunk)
         far[here, :] = (0.5 * (own[here, :].astype(F32) + far[here, :].astype(F32))).astype(BF16)
-        store = pltpu.make_async_copy(far.at[here], result.at[here], store_sem.at[index])
-        store.start()
-        stores.append(store)
+        pltpu.make_async_copy(far.at[here], result.at[here], store_sem.at[index]).start()
         copy.wait_send()
 
-    for chunk in range(CHUNKS):
-        mix(new_dn, far_dn, mixed_down, chunk, CHUNKS + chunk)
-    for chunk in range(CHUNKS):
-        mix(new_gu, far_gu, mixed_gate_up, chunk, chunk)
-    for chunk in range(CHUNKS):
+    each(CHUNKS, lambda chunk: mix(new_dn, far_dn, mixed_down, chunk, CHUNKS + chunk))
+    each(CHUNKS, lambda chunk: mix(new_gu, far_gu, mixed_gate_up, chunk, chunk))
+
+    def total_up(chunk):
         copy = back_copy(chunk)
         copy.wait_recv()
-        both = kept[:, span(chunk)].astype(F32) + arrived[:, span(chunk)].astype(F32)
-        kept[:, span(chunk)] = both.astype(BF16)
-        store = pltpu.make_async_copy(
-            kept.at[:, span(chunk)], token_grad.at[:, span(chunk)], store_sem.at[2 * CHUNKS + chunk]
-        )
-        store.start()
-        stores.append(store)
+        here = span(chunk)
+        both = across[0, :, here].astype(F32) + arrived[:, here].astype(F32)
+        arrived[:, here] = both.astype(BF16)
+        pltpu.make_async_copy(
+            arrived.at[:, here], token_grad.at[:, here], store_sem.at[2 * CHUNKS + chunk]
+        ).start()
         copy.wait_send()
+
+    each(CHUNKS, total_up)
     for part in range(2):
         all_sent_or_here(
             packed.at[1], rows.at[1], slice(None), x_send.at[2 + part], x_recv.at[0]
@@ -412,8 +429,17 @@
         all_sent_or_here(
             packed.at[0], returned, slice(None), ret_send.at[part], ret_recv.at[0]
         ).wait_send()
-    for store in stores:
-        store.wait()
+
+    def stored(chunk):
+        here = span(chunk)
+        for own, result, index in (
+            (far_dn.at[here], mixed_down.at[here], CHUNKS + chunk),
+            (far_gu.at[here], mixed_gate_up.at[here], chunk),
+            (arrived.at[:, here], token_grad.at[:, here], 2 * CHUNKS + chunk),
+        ):
+            pltpu.make_async_copy(own, result, store_sem.at[index]).wait()
+
+    each(CHUNKS, stored)
 
 
 def layer(level, experts, info, *arrays):
@@ -437,8 +463,7 @@
         out_specs=(anywhere,) * 3,
         scratch_shapes=[
             vmem(info.shape, F32),
-            vmem((2, tok_rows, width), BF16),
-            vmem((2, tok_rows, width), BF16),
+            vmem((2, 2, tok_rows, width), BF16),
             vmem((2, 2, part_rows, tok_rows), BF16),
             vmem((2, total, width), BF16),
             vmem((2, total, width), BF16),
@@ -455,8 +480,7 @@
             vmem((width, twice), BF16),
             vmem((width, single), BF16),
             vmem((total, width), BF16),
-            vmem((tok_rows, width), BF16),
-            vmem((tok_rows, width), BF16),
+            vmem((2, tok_rows, width), BF16),
             vmem((tok_rows, width), BF16),
             sems((6,)),
             sems((3 * CHUNKS,)),

time: 302 us -> 293 us (0.970)
  loops' own time: 6.73 us -> 0.37 us
    another operation x1, loops' own time: 6.73 us -> 0.37 us  [per_device(): lax.switch(level, [functools.partial(layer, at, experts) for at in range(...]
where the time goes in v2:
time: 293 us
  Pallas kernels  284 us (97%)
  local copies, waits for them, and re-layouts  3.98 us (1%)
    pallas_call x1, Pallas kernels, layer(): pl.pallas_call(functools.partial(layer_kernel, 1 << level, experts), out_...  284 us

profile of v2, /device:TPU:1, one launch (start us, length us, event | category | flops | bytes accessed | tf_op | source)
XLA Modules:
  0.0 292.8 jit_solution(6155077164531791085)
XLA Ops:
  2.6 0.1 pad.2.clone
  2.7 0.7 convert_bitcast_fusion.1
  3.3 0.7 convert_bitcast_fusion
  4.0 0.1 maximum_maximum_fusion
  4.1 284.8 %conditional.1 = ((bf16[256,2048]{1,0:T(8,128)(2,1)S(1)}, bf16[2048,512]{1,0:T(8,128)(2,1)S(1)}, bf16[2048,256]{1,0:T(8,128)(2,1)})) conditional(s32[]{:T(128)} %bitcast.24, (bf16[1,256,2048]{2,1,0:T(8,128)(2,1)}, bf16[1,256,2048]{2,1,0:T(8,128)(2,1)}, bf16[1,1,2048,512]{3,2,1,0:T(8,128)(2,1)}, ...), branch_computations={%region_0.0_spmd, %region_1.0_spmd, %region_2.0_spmd, %region_3.0_... | conditional | bytes 8 | solution.py:530
  4.3 284.4 %layer_shift_8.1 = (bf16[256,2048]{1,0:T(8,128)(2,1)S(1)}, bf16[2048,512]{1,0:T(8,128)(2,1)S(1)}, bf16[2048,256]{1,0:T(8,128)(2,1)}) custom-call(f32[8,256]{1,0:T(8,128)S(1)} %get-tuple-element.125.info, bf16[256,2048]{1,0:T(8,128)(2,1)} %bitcast.49, bf16[256,2048]{1,0:T(8,128)(2,1)} %bitcast.53, bf16[2048,512]{1,0:T(8,128)(2,1)} %bitcast.41, ...), custom_call_target="tpu_custom_call" | custom-call | tf_op jit(solution)/shard_map/cond/branch_3_fun/layer_shift_8/pallas_call | solution.py:455
  288.9 1.0 copy.27
  289.9 0.0 copy-start
  289.9 1.3 copy.28
  291.2 0.6 copy-done
  291.8 1.0 copy.29
  (1 shorter events, 0.0 us)
Async XLA Ops:
  289.9 2.0 copy-start

commit v3 on v2

--- a/solution.py
+++ b/solution.py
@@ -11,11 +11,11 @@
 STEP = 0.2
 DECAY = 0.9
 MESH = pl.DeviceIdType.MESH
-CHUNKS = 4
-AHEAD = 3
-FIRST = 2
-FORWARD_GAP = 3
-LATE = 6
+CHUNKS = 8
+FIRST = 8
+FORWARD_GAP = 2
+LATE = 10
+LAG = 3
 BF16 = jnp.bfloat16
 F32 = jnp.float32
 
@@ -29,16 +29,21 @@
 def layer_kernel(
     shift,
     experts,
-    info,
+    names,
+    shares,
     tokens,
     grads,
     gate_up,
     down,
     gate_up_velocity,
     down_velocity,
-    token_grad,
-    mixed_gate_up,
-    mixed_down,
+    out_gu,
+    far_gu,
+    out_dn,
+    far_dn,
+    kept,
+    arrived,
+    info,
     other_info,
     held,
     picks,
@@ -54,11 +59,8 @@
     pre_grad,
     new_gu,
     new_dn,
-    far_gu,
-    far_dn,
     returned,
     across,
-    arrived,
     load_sem,
     store_sem,
     z_send,
@@ -98,6 +100,10 @@
     def block(part, at):
         return pl.ds(pl.multiple_of(part * part_rows + at * capacity, capacity), capacity)
 
+    info[...] = jnp.zeros_like(info)
+    info[0:2, :] = names[...].astype(F32)
+    info[2:4, :] = shares[...].astype(F32)
+
     barrier = pltpu.get_barrier_semaphore()
     for step in range(1, group):
         pl.semaphore_signal(
@@ -139,8 +145,8 @@
         device_id_type=MESH,
     )
     info_copy.start()
-    for index in range(AHEAD):
-        z_copy(index, tokens).start()
+    for index in range(2 * CHUNKS):
+        z_copy(index, (tokens, grads)[index // CHUNKS]).start()
 
     def choose(part, table):
         names = [table[k : k + 1, :] for k in range(2)]
@@ -262,11 +268,6 @@
         copy = z_copy(index)
         copy.wait_recv()
         copy.wait_send()
-
-        @pl.when(index + AHEAD < 2 * CHUNKS)
-        def _():
-            z_copy(index + AHEAD).start()
-
         dispatch(index // CHUNKS, 1, index % CHUNKS)
 
     def swap_copy(source, target, at, count, index):
@@ -280,6 +281,9 @@
             device_id_type=MESH,
         )
 
+    def keep_copy(source, result, index):
+        return pltpu.make_async_copy(source, result, store_sem.at[index])
+
     def stepped(weight, velocity, gradient):
         return (
             weight.astype(F32) - STEP * (DECAY * velocity.astype(F32) + gradient)
@@ -302,6 +306,7 @@
 
         each(columns // 256, update)
         swap_copy(new_dn, far_dn, chunk, columns, CHUNKS + chunk).start()
+        keep_copy(new_dn.at[span(chunk)], out_dn.at[span(chunk)], 0).start()
 
     def dispatch_step(index):
         @pl.when(index < 2 * CHUNKS)
@@ -355,6 +360,7 @@
 
         each(columns // 256, update)
         swap_copy(new_gu, far_gu, chunk, columns, chunk).start()
+        keep_copy(new_gu.at[span(chunk)], out_gu.at[span(chunk)], 1).start()
 
     def wait_back(part, chunk):
         all_sent_or_here(
@@ -389,39 +395,33 @@
         def _():
             gate_up_chunk(index)
 
-        @pl.when(index >= CHUNKS)
-        def _():
-            combine(2 - index // CHUNKS, index % CHUNKS)
-
-        @pl.when((index >= CHUNKS) & (index < 2 * CHUNKS))
-        def _():
-            back_copy(index % CHUNKS).start()
-
-    each(3 * CHUNKS, return_step)
-
-    def mix(own, far, result, chunk, index):
-        copy = swap_copy(own, far, chunk, columns, index)
+        behind = index - LAG
+
+        @pl.when(behind >= 0)
+        def _():
+            combine(1 - behind // CHUNKS, behind % CHUNKS)
+
+        @pl.when(behind >= CHUNKS)
+        def _():
+            here = span(behind % CHUNKS)
+            keep_copy(across.at[0, :, here], kept.at[:, here], 2).start()
+
+        @pl.when((behind >= 0) & (behind < CHUNKS))
+        def _():
+            back_copy(behind % CHUNKS).start()
+
+    each(2 * CHUNKS + LAG, return_step)
+
+    def end(copy):
         copy.wait_recv()
-        here = span(chunk)
-        far[here, :] = (0.5 * (own[here, :].astype(F32) + far[here, :].astype(F32))).astype(BF16)
-        pltpu.make_async_copy(far.at[here], result.at[here], store_sem.at[index]).start()
         copy.wait_send()
 
-    each(CHUNKS, lambda chunk: mix(new_dn, far_dn, mixed_down, chunk, CHUNKS + chunk))
-    each(CHUNKS, lambda chunk: mix(new_gu, far_gu, mixed_gate_up, chunk, chunk))
-
-    def total_up(chunk):
-        copy = back_copy(chunk)
-        copy.wait_recv()
-        here = span(chunk)
-        both = across[0, :, here].astype(F32) + arrived[:, here].astype(F32)
-        arrived[:, here] = both.astype(BF16)
-        pltpu.make_async_copy(
-            arrived.at[:, here], token_grad.at[:, here], store_sem.at[2 * CHUNKS + chunk]
-        ).start()
-        copy.wait_send()
-
-    each(CHUNKS, total_up)
+    each(CHUNKS, lambda chunk: end(swap_copy(new_dn, far_dn, chunk, columns, CHUNKS + chunk)))
+    each(CHUNKS, lambda chunk: end(swap_copy(new_gu, far_gu, chunk, columns, chunk)))
+    each(CHUNKS, lambda chunk: end(back_copy(chunk)))
+    keep_copy(new_dn, out_dn, 0).wait()
+    keep_copy(new_gu, out_gu, 1).wait()
+    keep_copy(across.at[0], kept, 2).wait()
     for part in range(2):
         all_sent_or_here(
             packed.at[1], rows.at[1], slice(None), x_send.at[2 + part], x_recv.at[0]
@@ -430,19 +430,8 @@
             packed.at[0], returned, slice(None), ret_send.at[part], ret_recv.at[0]
         ).wait_send()
 
-    def stored(chunk):
-        here = span(chunk)
-        for own, result, index in (
-            (far_dn.at[here], mixed_down.at[here], CHUNKS + chunk),
-            (far_gu.at[here], mixed_gate_up.at[here], chunk),
-            (arrived.at[:, here], token_grad.at[:, here], 2 * CHUNKS + chunk),
-        ):
-            pltpu.make_async_copy(own, result, store_sem.at[index]).wait()
-
-    each(CHUNKS, stored)
-
-
-def layer(level, experts, info, *arrays):
+
+def layer(level, experts, names, shares, *arrays):
     tokens, _, gate_up, down = arrays[:4]
     tok_rows, width = tokens.shape
     twice = gate_up.shape[1]
@@ -455,14 +444,18 @@
     return pl.pallas_call(
         functools.partial(layer_kernel, 1 << level, experts),
         out_shape=(
-            jax.ShapeDtypeStruct((tok_rows, width), BF16),
+            jax.ShapeDtypeStruct((width, twice), BF16),
             jax.ShapeDtypeStruct((width, twice), BF16),
             jax.ShapeDtypeStruct((width, single), BF16),
+            jax.ShapeDtypeStruct((width, single), BF16),
+            jax.ShapeDtypeStruct((tok_rows, width), BF16),
+            jax.ShapeDtypeStruct((tok_rows, width), BF16),
         ),
-        in_specs=[pl.BlockSpec(memory_space=pltpu.VMEM)] + [anywhere] * 6,
-        out_specs=(anywhere,) * 3,
+        in_specs=[pl.BlockSpec(memory_space=pltpu.VMEM)] * 2 + [anywhere] * 6,
+        out_specs=(anywhere,) * 6,
         scratch_shapes=[
-            vmem(info.shape, F32),
+            vmem((8, tok_rows), F32),
+            vmem((8, tok_rows), F32),
             vmem((2, 2, tok_rows, width), BF16),
             vmem((2, 2, part_rows, tok_rows), BF16),
             vmem((2, total, width), BF16),
@@ -477,13 +470,10 @@
             vmem((total, twice), BF16),
             vmem((width, twice), BF16),
             vmem((width, single), BF16),
-            vmem((width, twice), BF16),
-            vmem((width, single), BF16),
             vmem((total, width), BF16),
             vmem((2, tok_rows, width), BF16),
-            vmem((tok_rows, width), BF16),
             sems((6,)),
-            sems((3 * CHUNKS,)),
+            sems((3,)),
             sems((2 * CHUNKS + 1,)),
             sems((2 * CHUNKS + 1,)),
             sems((4,)),
@@ -497,9 +487,9 @@
         ],
         name=f"layer_shift_{1 << level}",
         compiler_params=pltpu.CompilerParams(
-            collective_id=level, has_side_effects=True, vmem_limit_bytes=60 << 20
+            collective_id=level, has_side_effects=True, vmem_limit_bytes=48 << 20
         ),
-    )(info, *arrays)
+    )(names, shares, *arrays)
 
 
 def per_device(
@@ -515,22 +505,15 @@
 ):
     experts = lax.axis_size("expert")
     levels = lax.axis_size("replica").bit_length() - 1
-    info = jnp.concatenate(
-        [
-            routes[0].T.astype(F32),
-            route_weight[0].T.astype(F32),
-            jnp.zeros((4, tokens.shape[1]), F32),
-        ],
-        axis=0,
-    )
     shift = partner[0]
     level = jnp.zeros((), jnp.int32)
     for bit in range(levels):
         level = level + bit * jnp.bitwise_and(jnp.right_shift(shift, bit), 1)
-    token_grad, mixed_gate_up, mixed_down = lax.switch(
+    own_gu, far_gu, own_dn, far_dn, kept, arrived = lax.switch(
         level,
         [functools.partial(layer, at, experts) for at in range(levels)],
-        info,
+        routes[0].T,
+        route_weight[0].T,
         tokens[0],
         out_grad[0],
         gate_up_matrix[0, 0],
@@ -538,7 +521,12 @@
         gate_up_velocity[0, 0],
         down_velocity[0, 0],
     )
-    return token_grad[None], mixed_gate_up[None, None], mixed_down[None, None]
+
+    def mean(own, far):
+        return (0.5 * (own.astype(F32) + far.astype(F32))).astype(BF16)
+
+    token_grad = (kept.astype(F32) + arrived.astype(F32)).astype(BF16)
+    return token_grad[None], mean(own_gu, far_gu)[None, None], mean(own_dn, far_dn)[None, None]
 
 
 def solution(mesh):

time: 293 us -> 170 us (0.58)
  the two profiles are of different devices: /device:TPU:1 before, /device:TPU:32 now
where the time goes in v3:
time: 170 us
  Pallas kernels  162 us (95%)
  other arithmetic  4.62 us (3%)
  between operations  2.58 us (2%)
    pallas_call x1, Pallas kernels, layer(): pl.pallas_call(functools.partial(layer_kernel, 1 << level, experts), out_...  162 us

profile of v3, /device:TPU:32, one launch (start us, length us, event | category | flops | bytes accessed | tf_op | source)
XLA Modules:
  0.0 169.5 jit_solution(7640572232201583611)
XLA Ops:
  2.6 162.3 %conditional.1 = ((bf16[2048,512]{1,0:T(8,128)(2,1)S(1)}, bf16[2048,512]{1,0:T(8,128)(2,1)S(1)}, bf16[2048,256]{1,0:T(8,128)(2,1)S(1)}, bf16[2048,256]{1,0:T(8,1...) conditional(s32[]{:T(128)} %bitcast, ...), branch_computations={%region_0.0_spmd.clone, %region_1.0_spmd.clone, %region_2.0_spmd.c... | conditional | bytes 8 | solution.py:512
  2.6 162.3 %layer_shift_1.2 = (bf16[2048,512]{1,0:T(8,128)(2,1)S(1)}, bf16[2048,512]{1,0:T(8,128)(2,1)S(1)}, bf16[2048,256]{1,0:T(8,128)(2,1)S(1)}, bf16[2048,256]{1,0:T(8,...) custom-call(s32[2,256]{1,0:T(2,128)} %get-tuple-element.312.names, ...), custom_call_target="tpu_custom_call" | custom-call | tf_op jit(solution)/shard_map/cond/branch_0_fun/layer_shift_1/pallas_call | solution.py:444
  164.9 1.3 fusion.4
  166.2 1.4 fusion.5
  167.6 2.0 %fusion.1 = bf16[1,1,2048,512]{3,2,1,0:T(8,128)(2,1)} fusion(bf16[2048,512]{1,0:T(8,128)(2,1)S(1)} %get-tuple-element.387, bf16[2048,512]{1,0:T(8,128)(2,1)S(1)} %get-tuple-element.388), kind=kLoop, calls=%fused_computation.2 | loop fusion | flops 5242880 | bytes 6291456 | tf_op jit(solution)/shard_map/broadcast_in_dim | solution.py:529
